TPU v7x, 256 devices: a whole 4x4x8 slice. The times are simulated.
256 devices in a mesh: row: 8 (over z_hi, y), col: 32 (over x, z_lo, core).
Axes of the slice: x: 4, y: 4, z: 8 (z_hi: 2, z_lo: 4; z = z_hi * 4 + z_lo), core: 2. Of those that a mesh axis runs over, the one named last changes fastest.
Arguments:
- features: bfloat16 [65536, 256], P('col', 'row'), may hold values from -6 to 6
- block_values: bfloat16 [8, 32, 256, 128, 128], P('row', 'col'), may hold values from -0.046875 to 0.046875
- block_coords: int32 [8, 32, 2, 256], P('row', 'col'), may hold values from 0 to 63, as said below
- live_blocks: int32 [8, 32], P('row', 'col'), may hold values from 32 to 256, as said below
- weight: bfloat16 [256, 256], replicated, may hold values from -0.375 to 0.375
- bias: float32 [256], replicated, may hold values from -3 to 3
- cotangent: bfloat16 [65536, 256], P(('row', 'col')), may hold values from -6 to 6
Outputs:
- out: bfloat16 [65536, 256], P(('row', 'col'))
- grad_x: bfloat16 [65536, 256], P('col', 'row')
- grad_weight: float32 [256, 256], replicated
- grad_bias: float32 [256], replicated
Inputs may be any that keep to these rules, and one draw needn't show every extreme that they name: `block_coords`: within one tile the 256 slots name distinct pairs of a row block (0 to 63) and a column block (0 to 15). Only the first live_blocks[i, j] slots of tile (i, j) belong to the adjacency; some tile has all 256 slots live.
All inputs are finite; a program needn't handle non-finite values.
Results may differ from a plain program's by a relative error of at most 0.0075.
Values may be sent and summed in bfloat16 or wider, within the bound.
A program may use at most 128 MiB of HBM per device.

v0:
```python
import math
import jax
import jax.numpy as jnp
from jax import lax
from jax.sharding import PartitionSpec as P


def block_products(block_vals, source, dst_index, src_index, live_count, out_blocks, transposed):
    slot_total = block_vals.shape[0]
    block_size = block_vals.shape[1]
    feat_width = source.shape[2]
    group_size = math.gcd(slot_total, 64)
    pattern = "sab,saf->sbf" if transposed else "sab,sbf->saf"
    offsets = jnp.arange(group_size, dtype=jnp.int32)

    def one_group(turn, totals):
        first_slot = turn * group_size
        slab_vals = lax.dynamic_slice_in_dim(block_vals, first_slot, group_size, 0)
        take_from = lax.dynamic_slice_in_dim(src_index, first_slot, group_size, 0)
        put_to = lax.dynamic_slice_in_dim(dst_index, first_slot, group_size, 0)
        picked = jnp.take(source, take_from, axis=0)
        products = jnp.einsum(pattern, slab_vals, picked, preferred_element_type=jnp.float32)
        alive_mask = first_slot + offsets < live_count
        products = jnp.where(alive_mask[:, None, None], products, 0.0)
        return totals.at[put_to].add(products)

    start_totals = jnp.zeros((out_blocks, block_size, feat_width), jnp.float32)
    turns = slot_total // group_size
    return lax.fori_loop(0, turns, one_group, start_totals)


def on_device(features, block_values, block_coords, live_blocks, weight, bias, cotangent):
    block_vals = block_values[0, 0]
    row_ids = block_coords[0, 0, 0]
    col_ids = block_coords[0, 0, 1]
    live_count = live_blocks[0, 0]
    block_size = block_vals.shape[1]
    feat_width = weight.shape[0]
    col_count = lax.axis_size("col")
    feat_tile = lax.all_gather(features, "row", axis=1, tiled=True)
    col_blocks = feat_tile.shape[0] // block_size
    row_blocks = cotangent.shape[0] * col_count // block_size
    feat_blocks = feat_tile.reshape(col_blocks, block_size, feat_width)
    partial_value = block_products(
        block_vals, feat_blocks, row_ids, col_ids, live_count, row_blocks, False
    )
    partial_value = partial_value.reshape(row_blocks * block_size, feat_width)
    aggregate = lax.psum_scatter(partial_value, "col", scatter_dimension=0, tiled=True).astype(
        jnp.bfloat16
    )
    preact = jnp.dot(aggregate, weight, preferred_element_type=jnp.float32) + bias
    sigmoid_v = jax.nn.sigmoid(preact)
    out = (preact * sigmoid_v).astype(jnp.bfloat16)
    derivative = sigmoid_v * (1.0 + preact * (1.0 - sigmoid_v))
    grad_pre = (cotangent.astype(jnp.float32) * derivative).astype(jnp.bfloat16)
    weight_term = lax.dot_general(
        aggregate, grad_pre, (((0,), (0,)), ((), ())), preferred_element_type=jnp.float32
    )
    bias_term = jnp.sum(grad_pre.astype(jnp.float32), axis=0)
    weight_sum, bias_sum = lax.psum((weight_term, bias_term), ("row", "col"))
    norm_factor = (feat_tile.shape[0] * col_count) ** (-0.5)
    grad_weight = weight_sum * norm_factor
    grad_bias = bias_sum * norm_factor
    grad_agg = lax.dot_general(
        grad_pre, weight, (((1,), (1,)), ((), ())), preferred_element_type=jnp.float32
    ).astype(jnp.bfloat16)
    grad_tile = lax.all_gather(grad_agg, "col", axis=0, tiled=True)
    grad_blocks = grad_tile.reshape(row_blocks, block_size, feat_width)
    partial_x = block_products(
        block_vals, grad_blocks, col_ids, row_ids, live_count, col_blocks, True
    )
    partial_x = partial_x.reshape(col_blocks * block_size, feat_width)
    grad_x = lax.psum_scatter(partial_x, "row", scatter_dimension=1, tiled=True).astype(
        jnp.bfloat16
    )
    return (out, grad_x, grad_weight, grad_bias)


def solution(mesh):
    in_specs = (
        P("col", "row"),
        P("row", "col", None, None, None),
        P("row", "col", None, None),
        P("row", "col"),
        P(),
        P(),
        P(("row", "col"), None),
    )
    out_specs = (P(("row", "col"), None), P("col", "row"), P(), P())
    return jax.shard_map(
        on_device, mesh=mesh, in_specs=in_specs, out_specs=out_specs, check_vma=False
    )
```

profile of v0, /device:TPU:2, one launch (start us, length us, event | category | flops | bytes accessed | tf_op | source)
XLA Modules:
  0.0 785.1 jit_solution(2173765968436024874)
XLA Ops:
  7.2 0.7 all-gather.3.cloned.1.call-update
  8.0 0.8 fusion.27
  8.7 66.8 %all-gather.3.cloned.1.call-done = bf16[2048,256]{0,1:T(8,128)(2,1)} async-done(((bf16[2048,32]{0,1:T(8,128)(2,1)}), bf16[2048,256]{0,1:T(8,128)(2,1)}) %all-gather.3.cloned.1.call-update) | async-done | bytes 1048592 | tf_op jit(solution)/shard_map/all_gather | solution.py:40
  75.5 1.5 copy.12
  77.0 4.2 broadcast_in_dim.123
  81.3 122.0 %while.28 = (s32[]{:T(128)}, f32[64,128,256]{2,1,0:T(8,128)}, s32[256]{0:T(256)S(1)}, s32[]{:T(128)}, bf16[256,128,128]{2,1,0:T(8,128)(2,1)}, /*index=5*/s32[256...) while((s32[]{:T(128)}, f32[64,128,256]{2,1,0:T(8,128)}, ...), condition=%wide.region_2.3_spmd.clone, body=%wide.region_0.2_spmd.clone.sunk | while | flops 543164096 | bytes 48240816 | solution.py:29
  81.3 0.7 compare_and_fusion.4
  82.0 2.8 gather_fusion
  84.8 7.4 broadcast_select_fusion.4
  92.1 0.1 compare_select_fusion.8
  92.2 19.6 %scatter_fusion = f32[64,128,256]{2,1,0:T(8,128)} fusion(f32[64,128,256]{2,1,0:T(8,128)} %get-tuple-element.472, s32[64]{0:T(128)S(1)} %compare_select_fusion.8, f32[64,128,256]{2,1,0:T(8,128)} %broadcast_select_fusion.4), kind=kCustom, calls=%fused_computation.2.clone.clone.1 | custom fusion | flops 2097152 | bytes 25166080 | tf_op jit(solution)/shard_map/while/body/eval_jaxpr/scatter-add | solution.py:25
  111.8 0.7 compare_and_fusion.4
  112.6 2.8 gather_fusion
  115.3 7.4 broadcast_select_fusion.4
  122.7 0.1 compare_select_fusion.8
  122.8 19.4 %scatter_fusion = f32[64,128,256]{2,1,0:T(8,128)} fusion(f32[64,128,256]{2,1,0:T(8,128)} %get-tuple-element.472, s32[64]{0:T(128)S(1)} %compare_select_fusion.8, f32[64,128,256]{2,1,0:T(8,128)} %broadcast_select_fusion.4), kind=kCustom, calls=%fused_computation.2.clone.clone.1 | custom fusion | flops 2097152 | bytes 25166080 | tf_op jit(solution)/shard_map/while/body/eval_jaxpr/scatter-add | solution.py:25
  142.2 0.7 compare_and_fusion.4
  142.9 2.8 gather_fusion
  145.7 7.4 broadcast_select_fusion.4
  153.0 0.1 compare_select_fusion.8
  153.1 19.6 %scatter_fusion = f32[64,128,256]{2,1,0:T(8,128)} fusion(f32[64,128,256]{2,1,0:T(8,128)} %get-tuple-element.472, s32[64]{0:T(128)S(1)} %compare_select_fusion.8, f32[64,128,256]{2,1,0:T(8,128)} %broadcast_select_fusion.4), kind=kCustom, calls=%fused_computation.2.clone.clone.1 | custom fusion | flops 2097152 | bytes 25166080 | tf_op jit(solution)/shard_map/while/body/eval_jaxpr/scatter-add | solution.py:25
  172.7 0.7 compare_and_fusion.4
  173.5 2.8 gather_fusion
  176.2 7.4 broadcast_select_fusion.4
  183.6 0.1 compare_select_fusion.8
  183.6 19.6 %scatter_fusion = f32[64,128,256]{2,1,0:T(8,128)} fusion(f32[64,128,256]{2,1,0:T(8,128)} %get-tuple-element.472, s32[64]{0:T(128)S(1)} %compare_select_fusion.8, f32[64,128,256]{2,1,0:T(8,128)} %broadcast_select_fusion.4), kind=kCustom, calls=%fused_computation.2.clone.clone.1 | custom fusion | flops 2097152 | bytes 25166080 | tf_op jit(solution)/shard_map/while/body/eval_jaxpr/scatter-add | solution.py:25
  203.3 0.0 all-gather.5.cloned.1.call-start
  203.3 138.4 %reduce-scatter.3.cloned.1.call-done = f32[256,256]{1,0:T(8,128)} async-done(((f32[8192,256]{1,0:T(8,128)}), f32[256,256]{1,0:T(8,128)}) %reduce-scatter.3.cloned.1.call-update) | async-done | bytes 262160 | tf_op jit(solution)/shard_map/reduce_scatter | solution.py:48
  341.7 1.9 convert_reduce_fusion
  343.6 0.9 convolution_convert_fusion
  344.5 0.0 all-reduce.2.cloned.1.call-start
  344.6 12.0 %copy.11 = bf16[1,1,256,128,128]{3,4,2,1,0:T(8,128)(2,1)} copy(bf16[1,1,256,128,128]{4,3,2,1,0:T(8,128)(2,1)} %bitcast.18) | data formatting | bytes 16777216 | tf_op args[1]
  356.6 0.9 fusion.24
  357.5 0.0 reduce-scatter.5.cloned.1.call-start
  357.6 65.8 %all-gather.5.cloned.1.call-done = bf16[8192,256]{1,0:T(8,128)(2,1)} async-done(((bf16[256,256]{1,0:T(8,128)(2,1)}), bf16[8192,256]{1,0:T(8,128)(2,1)}) %all-gather.5.cloned.1.call-update) | async-done | bytes 4194320 | tf_op jit(solution)/shard_map/all_gather | solution.py:67
  423.4 0.2 broadcast_in_dim.124
  423.6 102.6 %while.29 = (s32[]{:T(128)}, f32[16,128,256]{2,1,0:T(8,128)S(1)}, s32[256]{0:T(256)S(1)}, s32[]{:T(128)}, bf16[256,128,128]{1,2,0:T(8,128)(2,1)}, /*index=5*/s32...) while((s32[]{:T(128)}, f32[16,128,256]{2,1,0:T(8,128)S(1)}, ...), condition=%wide.region_6.7_spmd.clone, body=%wide.region_4.6_spmd.clone.sunk | while | flops 543164096 | bytes 48240816 | solution.py:29
  423.7 0.7 compare_and_fusion.5
  424.4 5.0 gather_fusion.1
  429.4 7.4 broadcast_select_fusion.5
  436.7 0.1 compare_select_fusion.9
  436.8 12.4 %scatter_fusion.1 = f32[16,128,256]{2,1,0:T(8,128)S(1)} fusion(f32[16,128,256]{2,1,0:T(8,128)S(1)} %get-tuple-element.505, s32[64]{0:T(128)S(1)} %compare_select_fusion.9, f32[64,128,256]{2,1,0:T(8,128)} %broadcast_select_fusion.5), kind=kCustom, calls=%fused_computation.3.clone.clone.1 | custom fusion | flops 2097152 | bytes 25166080 | tf_op jit(solution)/shard_map/while/body/eval_jaxpr/scatter-add | solution.py:25
  449.3 0.7 compare_and_fusion.5
  450.0 5.0 gather_fusion.1
  455.0 7.4 broadcast_select_fusion.5
  462.4 0.1 compare_select_fusion.9
  462.5 12.5 %scatter_fusion.1 = f32[16,128,256]{2,1,0:T(8,128)S(1)} fusion(f32[16,128,256]{2,1,0:T(8,128)S(1)} %get-tuple-element.505, s32[64]{0:T(128)S(1)} %compare_select_fusion.9, f32[64,128,256]{2,1,0:T(8,128)} %broadcast_select_fusion.5), kind=kCustom, calls=%fused_computation.3.clone.clone.1 | custom fusion | flops 2097152 | bytes 25166080 | tf_op jit(solution)/shard_map/while/body/eval_jaxpr/scatter-add | solution.py:25
  475.0 0.7 compare_and_fusion.5
  475.7 5.0 gather_fusion.1
  480.7 7.4 broadcast_select_fusion.5
  488.1 0.1 compare_select_fusion.9
  488.2 12.4 %scatter_fusion.1 = f32[16,128,256]{2,1,0:T(8,128)S(1)} fusion(f32[16,128,256]{2,1,0:T(8,128)S(1)} %get-tuple-element.505, s32[64]{0:T(128)S(1)} %compare_select_fusion.9, f32[64,128,256]{2,1,0:T(8,128)} %broadcast_select_fusion.5), kind=kCustom, calls=%fused_computation.3.clone.clone.1 | custom fusion | flops 2097152 | bytes 25166080 | tf_op jit(solution)/shard_map/while/body/eval_jaxpr/scatter-add | solution.py:25
  500.6 0.7 compare_and_fusion.5
  501.3 5.0 gather_fusion.1
  506.3 7.4 broadcast_select_fusion.5
  513.7 0.1 compare_select_fusion.9
  513.8 12.4 %scatter_fusion.1 = f32[16,128,256]{2,1,0:T(8,128)S(1)} fusion(f32[16,128,256]{2,1,0:T(8,128)S(1)} %get-tuple-element.505, s32[64]{0:T(128)S(1)} %compare_select_fusion.9, f32[64,128,256]{2,1,0:T(8,128)} %broadcast_select_fusion.5), kind=kCustom, calls=%fused_computation.3.clone.clone.1 | custom fusion | flops 2097152 | bytes 25166080 | tf_op jit(solution)/shard_map/while/body/eval_jaxpr/scatter-add | solution.py:25
  526.2 1.9 copy.16
  528.1 76.1 %psum.15 = f32[256]{0:T(256)S(1)} all-reduce(f32[256]{0:T(256)S(1)} %get-tuple-element.355), channel_id=1, replica_groups=mesh['row'=8,'col'=32] {'row','col'}, use_global_device_ids=true, to_apply=%region_10.11 | all-reduce | flops 256 | bytes 2048 | tf_op jit(solution)/shard_map/psum | solution.py:60
  604.2 0.6 broadcast_multiply_fusion.1
  604.8 74.2 %all-reduce.2.cloned.1.call-done = f32[256,256]{1,0:T(8,128)} async-done(((f32[256,256]{1,0:T(8,128)}), f32[256,256]{1,0:T(8,128)}) %all-reduce.2.cloned.1.call-update) | async-done | bytes 262160 | tf_op jit(solution)/shard_map/psum | solution.py:60
  679.0 1.7 broadcast_multiply_fusion
  680.7 96.3 %reduce-scatter.5.cloned.1.call-done = f32[2048,32]{0,1:T(8,128)} async-done(((f32[2048,256]{0,1:T(8,128)}), f32[2048,32]{0,1:T(8,128)}) %reduce-scatter.5.cloned.1.call-update) | async-done | bytes 262160 | tf_op jit(solution)/shard_map/reduce_scatter | solution.py:73
  776.9 1.6 convert_element_type.26
  (22 shorter events, 0.2 us)
Async XLA Ops:
  7.2 334.6 %copy-start = (bf16[256,256]{1,0:T(8,128)(2,1)S(1)}, bf16[256,256]{1,0:T(8,128)(2,1)}, u32[]{:S(2)}) copy-start(bf16[256,256]{1,0:T(8,128)(2,1)} %param.15) | copy-start | bytes 393220
  7.2 68.4 %all-gather.3.cloned.1.call-start = ((), (), s32[]{:S(2)}) async-start(), calls=%async_computation.2 | async-start | bytes 1179648 | tf_op jit(solution)/shard_map/all_gather | solution.py:40
  7.9 333.8 %reduce-scatter.3.cloned.1.call-start = ((), (), s32[]{:S(2)}) async-start(), calls=%async_computation.3 | async-start | bytes 8650752 | tf_op jit(solution)/shard_map/reduce_scatter | solution.py:48
  203.3 138.5 %copy-start.2 = (bf16[256,256]{1,0:T(8,128)(2,1)S(1)}, bf16[256,256]{1,0:T(8,128)(2,1)}, u32[]{:S(2)}) copy-start(bf16[256,256]{1,0:T(8,128)(2,1)} %param.17) | copy-start | bytes 393220
  203.3 138.5 %copy-start.3 = (f32[256]{0:T(256)S(1)}, f32[256]{0:T(256)}, u32[]{:S(2)}) copy-start(f32[256]{0:T(256)} %param.16) | copy-start | bytes 3076
  203.3 220.1 %all-gather.5.cloned.1.call-start = ((), (), s32[]{:S(2)}) async-start(), calls=%async_computation.4 | async-start | bytes 4325376 | tf_op jit(solution)/shard_map/all_gather | solution.py:67
  344.5 12.1 %copy-start.1 = (f32[256,256]{1,0:T(8,128)S(1)}, f32[256,256]{1,0:T(8,128)}, u32[]{:S(2)}) copy-start(f32[256,256]{1,0:T(8,128)} %reduce-scatter.3.cloned.1.call-done) | copy-start | bytes 786436
  344.5 334.4 %all-reduce.2.cloned.1.call-start = ((), (), s32[]{:S(2)}) async-start(), calls=%async_computation.6 | async-start | bytes 524288 | tf_op jit(solution)/shard_map/psum | solution.py:60
  357.5 419.4 %reduce-scatter.5.cloned.1.call-start = ((), (), s32[]{:S(2)}) async-start(), calls=%async_computation.5 | async-start | bytes 2359296 | tf_op jit(solution)/shard_map/reduce_scatter | solution.py:73
Sparse Core Ops, SparseCore 0:
  10.6 64.8 all-gather.2
  203.4 138.2 reduce-scatter.2
  344.7 78.7 all-gather.4
  429.3 249.6 all-reduce.1
  682.9 93.9 reduce-scatter.4
where the time goes:
time: 787 us; the launch traced here: 785 us
  waiting for transfers between devices  442 us (56%)
  other arithmetic  138 us (18%)
  blocking collectives  76.1 us (10%)
  matrix products  62.7 us (8%)
  local copies, waits for them, and re-layouts  51.5 us (7%)
  between operations  13.8 us (2%)
    reduce_scatter x1, waiting for transfers between devices, on_device(): lax.psum_scatter(partial_value, 'col', scatter_dimension=0, tiled=True)  138 us
    scatter-add x8, other arithmetic, one_group(): return totals.at[put_to].add(products)  128 us
    reduce_scatter x1, waiting for transfers between devices, on_device(): lax.psum_scatter(partial_x, 'row', scatter_dimension=1, tiled=True)  96.3 us
    psum x1, blocking collectives, on_device(): weight_sum, bias_sum = lax.psum((weight_term, bias_term), ('row', 'col'))  76.1 us
    psum x1, waiting for transfers between devices, on_device(): weight_sum, bias_sum = lax.psum((weight_term, bias_term), ('row', 'col'))  74.2 us
    all_gather x1, waiting for transfers between devices, on_device(): feat_tile = lax.all_gather(features, 'row', axis=1, tiled=True)  66.8 us
    all_gather x1, waiting for transfers between devices, on_device(): grad_tile = lax.all_gather(grad_agg, 'col', axis=0, tiled=True)  65.8 us
    dot_general x8, matrix products, one_group(): jnp.einsum(pattern, slab_vals, picked, preferred_element_type=jnp.float32)  59 us
  transfers between devices with their start and end apart: 5, of which 5 were waited for; matrix products, arithmetic and copies ran while one was open for 15% of the time, Pallas kernels for 0%

commit v1 on v0

--- a/solution.py
+++ b/solution.py
@@ -3,6 +3,11 @@
 import jax.numpy as jnp
 from jax import lax
 from jax.sharding import PartitionSpec as P
+
+
+def by_each_axis(array, inner_axis, outer_axis):
+    inner = lax.psum(array, inner_axis)
+    return lax.psum(inner, outer_axis)
 
 
 def block_products(block_vals, source, dst_index, src_index, live_count, out_blocks, transposed):
@@ -57,7 +62,7 @@
         aggregate, grad_pre, (((0,), (0,)), ((), ())), preferred_element_type=jnp.float32
     )
     bias_term = jnp.sum(grad_pre.astype(jnp.float32), axis=0)
-    weight_sum, bias_sum = lax.psum((weight_term, bias_term), ("row", "col"))
+    weight_sum, bias_sum = by_each_axis((weight_term, bias_term), "row", "col")
     norm_factor = (feat_tile.shape[0] * col_count) ** (-0.5)
     grad_weight = weight_sum * norm_factor
     grad_bias = bias_sum * norm_factor

time: 787 us -> 913 us (1.16)
  waiting for transfers between devices: 442 us -> 556 us
  blocking collectives: 76.1 us -> 87.6 us
    psum x1 -> x2, waiting for transfers between devices: 74.2 us -> 180 us  [the longest x1 110 us: by_each_axis(): inner = lax.psum(array, inner_axis)]
    reduce_scatter x1, waiting for transfers between devices: 96.3 us -> 109 us  [on_device(): lax.psum_scatter(partial_x, 'row', scatter_dimension=1, tiled=True)]
    psum x1 -> x2, blocking collectives: 76.1 us -> 87.6 us  [the longest x1 57.7 us: by_each_axis(): return lax.psum(inner, outer_axis)]
  transfers between devices with their start and end apart: 5 -> 6, of which waited for: 5 -> 6; matrix products, arithmetic and copies ran while one was open for 15% -> 13% of each run, Pallas kernels for 0% -> 0%
where the time goes in v1:
time: 913 us; the launch traced here: 911 us
  waiting for transfers between devices  556 us (61%)
  other arithmetic  138 us (15%)
  blocking collectives  87.6 us (10%)
  matrix products  63.6 us (7%)
  local copies, waits for them, and re-layouts  51.4 us (6%)
  between operations  14.2 us (2%)
    reduce_scatter x1, waiting for transfers between devices, on_device(): lax.psum_scatter(partial_value, 'col', scatter_dimension=0, tiled=True)  139 us
    scatter-add x8, other arithmetic, one_group(): return totals.at[put_to].add(products)  128 us
    psum x1, waiting for transfers between devices, by_each_axis(): inner = lax.psum(array, inner_axis)  110 us
    reduce_scatter x1, waiting for transfers between devices, on_device(): lax.psum_scatter(partial_x, 'row', scatter_dimension=1, tiled=True)  109 us
    psum x1, waiting for transfers between devices, by_each_axis(): return lax.psum(inner, outer_axis)  69.7 us
    all_gather x1, waiting for transfers between devices, on_device(): feat_tile = lax.all_gather(features, 'row', axis=1, tiled=True)  66.8 us
    all_gather x1, waiting for transfers between devices, on_device(): grad_tile = lax.all_gather(grad_agg, 'col', axis=0, tiled=True)  60.3 us
    dot_general x8, matrix products, one_group(): jnp.einsum(pattern, slab_vals, picked, preferred_element_type=jnp.float32)  59 us
  transfers between devices with their start and end apart: 6, of which 6 were waited for; matrix products, arithmetic and copies ran while one was open for 13% of the time, Pallas kernels for 0%

profile of v1, /device:TPU:2, one launch (start us, length us, event | category | flops | bytes accessed | tf_op | source)
XLA Modules:
  0.0 911.4 jit_solution(9639546746695550001)
XLA Ops:
  7.2 0.7 all-gather.3.cloned.1.call-update
  8.0 0.8 fusion.27
  8.7 66.8 %all-gather.3.cloned.1.call-done = bf16[2048,256]{0,1:T(8,128)(2,1)} async-done(((bf16[2048,32]{0,1:T(8,128)(2,1)}), bf16[2048,256]{0,1:T(8,128)(2,1)}) %all-gather.3.cloned.1.call-update) | async-done | bytes 1048592 | tf_op jit(solution)/shard_map/all_gather | solution.py:45
  75.5 1.5 copy.12
  77.0 4.2 broadcast_in_dim.123
  81.3 122.1 %while.28 = (s32[]{:T(128)}, f32[64,128,256]{2,1,0:T(8,128)}, s32[256]{0:T(256)S(1)}, s32[]{:T(128)}, bf16[256,128,128]{2,1,0:T(8,128)(2,1)}, /*index=5*/s32[256...) while((s32[]{:T(128)}, f32[64,128,256]{2,1,0:T(8,128)}, ...), condition=%wide.region_2.3_spmd.clone, body=%wide.region_0.2_spmd.clone.sunk | while | flops 543164096 | bytes 48240816 | solution.py:34
  81.3 0.7 compare_and_fusion.4
  82.0 2.8 gather_fusion
  84.7 7.4 broadcast_select_fusion.4
  92.1 0.1 compare_select_fusion.8
  92.2 19.7 %scatter_fusion = f32[64,128,256]{2,1,0:T(8,128)} fusion(f32[64,128,256]{2,1,0:T(8,128)} %get-tuple-element.472, s32[64]{0:T(128)S(1)} %compare_select_fusion.8, f32[64,128,256]{2,1,0:T(8,128)} %broadcast_select_fusion.4), kind=kCustom, calls=%fused_computation.2.clone.clone.1 | custom fusion | flops 2097152 | bytes 25166080 | tf_op jit(solution)/shard_map/while/body/eval_jaxpr/scatter-add | solution.py:30
  111.9 0.7 compare_and_fusion.4
  112.6 2.8 gather_fusion
  115.4 7.4 broadcast_select_fusion.4
  122.7 0.1 compare_select_fusion.8
  122.8 19.6 %scatter_fusion = f32[64,128,256]{2,1,0:T(8,128)} fusion(f32[64,128,256]{2,1,0:T(8,128)} %get-tuple-element.472, s32[64]{0:T(128)S(1)} %compare_select_fusion.8, f32[64,128,256]{2,1,0:T(8,128)} %broadcast_select_fusion.4), kind=kCustom, calls=%fused_computation.2.clone.clone.1 | custom fusion | flops 2097152 | bytes 25166080 | tf_op jit(solution)/shard_map/while/body/eval_jaxpr/scatter-add | solution.py:30
  142.5 0.7 compare_and_fusion.4
  143.2 2.8 gather_fusion
  145.9 7.4 broadcast_select_fusion.4
  153.3 0.1 compare_select_fusion.8
  153.4 19.6 %scatter_fusion = f32[64,128,256]{2,1,0:T(8,128)} fusion(f32[64,128,256]{2,1,0:T(8,128)} %get-tuple-element.472, s32[64]{0:T(128)S(1)} %compare_select_fusion.8, f32[64,128,256]{2,1,0:T(8,128)} %broadcast_select_fusion.4), kind=kCustom, calls=%fused_computation.2.clone.clone.1 | custom fusion | flops 2097152 | bytes 25166080 | tf_op jit(solution)/shard_map/while/body/eval_jaxpr/scatter-add | solution.py:30
  173.0 0.7 compare_and_fusion.4
  173.7 2.8 gather_fusion
  176.5 7.4 broadcast_select_fusion.4
  183.8 0.1 compare_select_fusion.8
  183.9 19.5 %scatter_fusion = f32[64,128,256]{2,1,0:T(8,128)} fusion(f32[64,128,256]{2,1,0:T(8,128)} %get-tuple-element.472, s32[64]{0:T(128)S(1)} %compare_select_fusion.8, f32[64,128,256]{2,1,0:T(8,128)} %broadcast_select_fusion.4), kind=kCustom, calls=%fused_computation.2.clone.clone.1 | custom fusion | flops 2097152 | bytes 25166080 | tf_op jit(solution)/shard_map/while/body/eval_jaxpr/scatter-add | solution.py:30
  203.4 138.6 %reduce-scatter.3.cloned.1.call-done = f32[256,256]{1,0:T(8,128)} async-done(((f32[8192,256]{1,0:T(8,128)}), f32[256,256]{1,0:T(8,128)}) %reduce-scatter.3.cloned.1.call-update) | async-done | bytes 262160 | tf_op jit(solution)/shard_map/reduce_scatter | solution.py:53
  342.1 1.9 convert_reduce_fusion
  344.0 1.9 fusion.24
  345.9 0.0 all-gather.5.cloned.1.call-start
  345.9 0.9 convolution_convert_fusion
  346.9 12.0 %copy.11 = bf16[1,1,256,128,128]{3,4,2,1,0:T(8,128)(2,1)} copy(bf16[1,1,256,128,128]{4,3,2,1,0:T(8,128)(2,1)} %bitcast.18) | data formatting | bytes 16777216 | tf_op args[1]
  358.8 110.1 %all-reduce.3.cloned.1.call-done = f32[256,256]{1,0:T(8,128)} async-done(((f32[256,256]{1,0:T(8,128)}), f32[256,256]{1,0:T(8,128)}) %all-reduce.3.cloned.1.call-update) | async-done | bytes 262160 | tf_op jit(solution)/shard_map/psum | solution.py:9
  469.0 60.3 %all-gather.5.cloned.1.call-done = bf16[8192,256]{1,0:T(8,128)(2,1)} async-done(((bf16[256,256]{1,0:T(8,128)(2,1)}), bf16[8192,256]{1,0:T(8,128)(2,1)}) %all-gather.5.cloned.1.call-update) | async-done | bytes 4194320 | tf_op jit(solution)/shard_map/all_gather | solution.py:72
  529.3 0.2 broadcast_in_dim.124
  529.5 102.5 %while.29 = (s32[]{:T(128)}, f32[16,128,256]{2,1,0:T(8,128)S(1)}, s32[256]{0:T(256)S(1)}, s32[]{:T(128)}, bf16[256,128,128]{1,2,0:T(8,128)(2,1)}, /*index=5*/s32...) while((s32[]{:T(128)}, f32[16,128,256]{2,1,0:T(8,128)S(1)}, ...), condition=%wide.region_6.7_spmd.clone, body=%wide.region_4.6_spmd.clone.sunk | while | flops 543164096 | bytes 48240816 | solution.py:34
  529.5 0.7 compare_and_fusion.5
  530.3 5.0 gather_fusion.1
  535.2 7.4 broadcast_select_fusion.5
  542.6 0.1 compare_select_fusion.9
  542.7 12.4 %scatter_fusion.1 = f32[16,128,256]{2,1,0:T(8,128)S(1)} fusion(f32[16,128,256]{2,1,0:T(8,128)S(1)} %get-tuple-element.505, s32[64]{0:T(128)S(1)} %compare_select_fusion.9, f32[64,128,256]{2,1,0:T(8,128)} %broadcast_select_fusion.5), kind=kCustom, calls=%fused_computation.3.clone.clone.1 | custom fusion | flops 2097152 | bytes 25166080 | tf_op jit(solution)/shard_map/while/body/eval_jaxpr/scatter-add | solution.py:30
  555.1 0.7 compare_and_fusion.5
  555.9 5.0 gather_fusion.1
  560.9 7.4 broadcast_select_fusion.5
  568.3 0.1 compare_select_fusion.9
  568.3 12.5 %scatter_fusion.1 = f32[16,128,256]{2,1,0:T(8,128)S(1)} fusion(f32[16,128,256]{2,1,0:T(8,128)S(1)} %get-tuple-element.505, s32[64]{0:T(128)S(1)} %compare_select_fusion.9, f32[64,128,256]{2,1,0:T(8,128)} %broadcast_select_fusion.5), kind=kCustom, calls=%fused_computation.3.clone.clone.1 | custom fusion | flops 2097152 | bytes 25166080 | tf_op jit(solution)/shard_map/while/body/eval_jaxpr/scatter-add | solution.py:30
  580.8 0.7 compare_and_fusion.5
  581.6 5.0 gather_fusion.1
  586.5 7.4 broadcast_select_fusion.5
  593.9 0.1 compare_select_fusion.9
  594.0 12.4 %scatter_fusion.1 = f32[16,128,256]{2,1,0:T(8,128)S(1)} fusion(f32[16,128,256]{2,1,0:T(8,128)S(1)} %get-tuple-element.505, s32[64]{0:T(128)S(1)} %compare_select_fusion.9, f32[64,128,256]{2,1,0:T(8,128)} %broadcast_select_fusion.5), kind=kCustom, calls=%fused_computation.3.clone.clone.1 | custom fusion | flops 2097152 | bytes 25166080 | tf_op jit(solution)/shard_map/while/body/eval_jaxpr/scatter-add | solution.py:30
  606.5 0.7 compare_and_fusion.5
  607.2 5.0 gather_fusion.1
  612.2 7.4 broadcast_select_fusion.5
  619.5 0.1 compare_select_fusion.9
  619.6 12.4 %scatter_fusion.1 = f32[16,128,256]{2,1,0:T(8,128)S(1)} fusion(f32[16,128,256]{2,1,0:T(8,128)S(1)} %get-tuple-element.505, s32[64]{0:T(128)S(1)} %compare_select_fusion.9, f32[64,128,256]{2,1,0:T(8,128)} %broadcast_select_fusion.5), kind=kCustom, calls=%fused_computation.3.clone.clone.1 | custom fusion | flops 2097152 | bytes 25166080 | tf_op jit(solution)/shard_map/while/body/eval_jaxpr/scatter-add | solution.py:30
  632.1 1.9 copy.16
  634.0 30.0 %psum.30 = f32[256]{0:T(256)S(1)} all-reduce(f32[256]{0:T(256)S(1)} %get-tuple-element.355), channel_id=1, replica_groups=mesh['row'=8,'col'=32] {'row'}, use_global_device_ids=true, to_apply=%region_11.12 | all-reduce | flops 256 | bytes 2048 | tf_op jit(solution)/shard_map/psum | solution.py:9
  663.9 57.7 %psum.31 = f32[256]{0:T(256)S(1)} all-reduce(f32[256]{0:T(256)S(1)} %psum.30), channel_id=1, replica_groups=mesh['row'=8,'col'=32] {'col'}, use_global_device_ids=true, to_apply=%region_12.13 | all-reduce | flops 256 | bytes 2048 | tf_op jit(solution)/shard_map/psum | solution.py:10
  721.6 0.6 broadcast_multiply_fusion.1
  722.2 69.7 %all-reduce.5.cloned.1.call-done = f32[256,256]{1,0:T(8,128)} async-done(((f32[256,256]{1,0:T(8,128)}), f32[256,256]{1,0:T(8,128)}) %all-reduce.5.cloned.1.call-update) | async-done | bytes 262160 | tf_op jit(solution)/shard_map/psum | solution.py:10
  791.9 1.7 broadcast_multiply_fusion
  793.6 109.4 %reduce-scatter.5.cloned.1.call-done = f32[2048,32]{0,1:T(8,128)} async-done(((f32[2048,256]{0,1:T(8,128)}), f32[2048,32]{0,1:T(8,128)}) %reduce-scatter.5.cloned.1.call-update) | async-done | bytes 262160 | tf_op jit(solution)/shard_map/reduce_scatter | solution.py:78
  903.0 1.6 convert_element_type.26
  (24 shorter events, 0.3 us)
Async XLA Ops:
  7.2 334.9 %copy-start = (bf16[256,256]{1,0:T(8,128)(2,1)S(1)}, bf16[256,256]{1,0:T(8,128)(2,1)}, u32[]{:S(2)}) copy-start(bf16[256,256]{1,0:T(8,128)(2,1)} %param.15) | copy-start | bytes 393220
  7.2 68.4 %all-gather.3.cloned.1.call-start = ((), (), s32[]{:S(2)}) async-start(), calls=%async_computation.2 | async-start | bytes 1179648 | tf_op jit(solution)/shard_map/all_gather | solution.py:45
  7.9 334.1 %reduce-scatter.3.cloned.1.call-start = ((), (), s32[]{:S(2)}) async-start(), calls=%async_computation.3 | async-start | bytes 8650752 | tf_op jit(solution)/shard_map/reduce_scatter | solution.py:53
  203.4 138.7 %copy-start.1 = (bf16[256,256]{1,0:T(8,128)(2,1)S(1)}, bf16[256,256]{1,0:T(8,128)(2,1)}, u32[]{:S(2)}) copy-start(bf16[256,256]{1,0:T(8,128)(2,1)} %param.17) | copy-start | bytes 393220
  203.4 138.7 %copy-start.2 = (f32[256]{0:T(256)S(1)}, f32[256]{0:T(256)}, u32[]{:S(2)}) copy-start(f32[256]{0:T(256)} %param.16) | copy-start | bytes 3076
  203.4 265.5 %all-reduce.3.cloned.1.call-start = ((), (), s32[]{:S(2)}) async-start(), calls=%async_computation.6 | async-start | bytes 524288 | tf_op jit(solution)/shard_map/psum | solution.py:9
  345.9 183.5 %all-gather.5.cloned.1.call-start = ((), (), s32[]{:S(2)}) async-start(), calls=%async_computation.4 | async-start | bytes 4325376 | tf_op jit(solution)/shard_map/all_gather | solution.py:72
  346.8 445.1 %all-reduce.5.cloned.1.call-start = ((), (), s32[]{:S(2)}) async-start(), calls=%async_computation.7 | async-start | bytes 524288 | tf_op jit(solution)/shard_map/psum | solution.py:10
  469.0 434.0 %reduce-scatter.5.cloned.1.call-start = ((), (), s32[]{:S(2)}) async-start(), calls=%async_computation.5 | async-start | bytes 2359296 | tf_op jit(solution)/shard_map/reduce_scatter | solution.py:78
Sparse Core Ops, SparseCore 0:
  10.6 64.8 all-gather.2
  203.5 138.4 reduce-scatter.2
  346.0 122.9 all-reduce.2
  471.4 57.8 all-gather.4
  532.0 259.9 all-reduce.4
  795.8 107.0 reduce-scatter.4
